TPU v7x, 32 devices: a whole 2x2x4 slice. The times are simulated.
32 devices in a mesh: grp: 2 (over y), mk: 4 (over z), pp: 2 (over x), sub: 2 (over core).
Axes of the slice: x: 2, y: 2, z: 4, core: 2. Of those that a mesh axis runs over, the one named last changes fastest.
Arguments:
- genotypes: bfloat16 [4096, 16384], P(('grp', 'pp', 'sub'), 'mk'), parts along dimension 0, may hold values from -6 to 6
- estimate: bfloat16 [512, 16384], P(('grp', 'pp', 'sub'), 'mk'), parts along dimension 0, may hold values from -0.046875 to 0.046875
- phenotypes: bfloat16 [512, 2048], P('grp', ('pp', 'sub')), parts along dimension 0, may hold values from -6 to 6
- prior_logit: float32 [512], P(('grp', 'pp', 'sub')), parts along dimension 0, may hold values from -2 to 1
- slab_var: float32 [512], P(('grp', 'pp', 'sub')), parts along dimension 0, may hold values from 0.5 to 4
- noise_var: float32 [512], P(('grp', 'pp', 'sub')), parts along dimension 0, may hold values from 0.5 to 2
- tile_chrom: int32 [64], P('grp'), parts along dimension 0, may hold values from 0 to 21, as said below
Outputs:
- updated: bfloat16 [512, 16384], P(('grp', 'pp', 'sub'), 'mk'), parts along dimension 0
- loco_out: bfloat16 [44, 256, 2048], P('grp', 'mk', ('pp', 'sub')), parts along dimension 0
There are 2 independent parts, one for each index of `grp`. A program takes and returns all parts, laid end to end along the dimension named above; each array names one. Nothing has to cross between parts.
Inputs may be any that keep to these rules, and one draw needn't show every extreme that they name: `tile_chrom`: never falling along the tiles; every chromosome owns at least one tile; the tiles of one device (aligned blocks of 8 tiles) name at most 6 chromosomes, and some device names exactly 6.
All inputs are finite; a program needn't handle non-finite values.
Results may differ from a plain program's by a relative error of at most 0.0059.
Values may be sent and summed in bfloat16 or wider, within the bound.
A program may use at most 64 MiB of HBM per device.

v0:
```python
import math

import jax
import jax.numpy as jnp
from jax import lax
from jax.sharding import PartitionSpec as P

CHROMS = 22
TILE = 512
SPAN = 6


def denoise(estimate, scores, prior_logit, slab_var, noise_var, marker_root, people_root):
    observed = marker_root * estimate.astype(jnp.float32) + scores * (1.0 / people_root)
    slab_col = slab_var[:, None]
    noise_col = noise_var[:, None]
    spread = slab_col + noise_col
    log_odds = (
        prior_logit[:, None]
        + 0.5 * jnp.log(noise_col / spread)
        + 0.5 * observed * observed * (1.0 / noise_col - 1.0 / spread)
    )
    posterior = jax.nn.sigmoid(log_odds) * (slab_col / spread) * observed
    return (posterior * (1.0 / marker_root)).astype(jnp.bfloat16)


def per_device(genotypes, estimate, phenotypes, prior_logit, slab_var, noise_var, tile_chrom):
    people_dev, mark_dev = genotypes.shape
    mk_count = lax.axis_size("mk")
    people_count = lax.axis_size(("pp", "sub"))
    traits = phenotypes.shape[0]
    partial_pred = lax.dot_general(
        lax.all_gather(estimate, ("pp", "sub"), axis=0, tiled=True),
        genotypes,
        (((1,), (1,)), ((), ())),
        preferred_element_type=jnp.float32,
    )
    share_rows = traits // mk_count
    offset = lax.axis_index("mk") * share_rows
    phen_share = lax.dynamic_slice_in_dim(phenotypes, offset, share_rows, 0).astype(jnp.float32)
    prediction = lax.psum(partial_pred, "mk")
    residual = (phenotypes.astype(jnp.float32) - prediction).astype(jnp.bfloat16)
    scores = lax.psum_scatter(
        jnp.dot(residual, genotypes, preferred_element_type=jnp.float32),
        ("pp", "sub"),
        scatter_dimension=0,
        tiled=True,
    )
    updated = denoise(
        estimate,
        scores,
        prior_logit,
        slab_var,
        noise_var,
        math.sqrt(mark_dev * mk_count),
        math.sqrt(people_dev * people_count),
    )
    tile_dev = mark_dev // TILE
    own_tiles = lax.dynamic_slice_in_dim(tile_chrom, lax.axis_index("mk") * tile_dev, tile_dev, 0)
    labels = own_tiles[0] + jnp.arange(SPAN, dtype=jnp.int32)
    member = (labels[:, None] == own_tiles[None, :]).astype(jnp.float32)
    geno_tiles = genotypes.reshape(people_dev, tile_dev, TILE)
    shard_rows = lax.all_gather(updated, ("pp", "sub"), axis=0, tiled=True)
    tile_terms = jnp.einsum(
        "kta,pta->tkp",
        shard_rows.reshape(shard_rows.shape[0], tile_dev, TILE),
        geno_tiles,
        preferred_element_type=jnp.float32,
    )
    local_sums = jnp.einsum("st,tkp->skp", member, tile_terms, precision=lax.Precision.HIGHEST)
    received = lax.all_to_all(local_sums, "mk", split_axis=1, concat_axis=0, tiled=True)
    firsts = tile_chrom.reshape(mk_count, tile_dev)[:, 0]
    sources = (firsts[:, None] + jnp.arange(SPAN, dtype=jnp.int32)[None, :]).reshape(-1)
    assign = (jnp.arange(CHROMS, dtype=jnp.int32)[:, None] == sources[None, :]).astype(jnp.float32)
    chrom_sums = jnp.einsum("cj,jkp->ckp", assign, received, precision=lax.Precision.HIGHEST)
    combined = jnp.sum(chrom_sums, axis=0)
    loco_out = (phen_share[None] - combined[None] + chrom_sums).astype(jnp.bfloat16)
    return (updated, loco_out)


def solution(mesh):
    placed = (
        P(("grp", "pp", "sub"), "mk"),
        P(("grp", "pp", "sub"), "mk"),
        P("grp", ("pp", "sub")),
        P(("grp", "pp", "sub")),
        P(("grp", "pp", "sub")),
        P(("grp", "pp", "sub")),
        P("grp"),
    )
    return jax.shard_map(
        per_device,
        mesh=mesh,
        in_specs=placed,
        out_specs=(P(("grp", "pp", "sub"), "mk"), P("grp", "mk", ("pp", "sub"))),
        check_vma=False,
    )
```

profile of v0, /device:TPU:0, one launch (start us, length us, event | category | flops | bytes accessed | tf_op | source)
XLA Modules:
  0.0 279.5 jit_solution(18358932344819804699)
XLA Ops:
  7.2 0.0 all-gather.3.cloned.1.call-start
  7.2 0.7 all-gather.3.cloned.1.call-update
  7.9 0.0 all-reduce.2.cloned.1.call-start
  8.0 26.9 %all-gather.3.cloned.1.call-done = bf16[256,4096]{1,0:T(8,128)(2,1)} async-done(((bf16[64,4096]{1,0:T(8,128)(2,1)}), bf16[256,4096]{1,0:T(8,128)(2,1)}) %all-gather.3.cloned.1.call-update) | async-done | bytes 2097168 | tf_op jit(solution)/shard_map/all_gather | solution.py:33
  34.8 4.9 %fusion.26 = f32[256,512]{1,0:T(8,128)} fusion(bf16[256,4096]{1,0:T(8,128)(2,1)} %all-gather.3.cloned.1.call-done, bf16[512,4096]{1,0:T(8,128)(2,1)} %param.7), kind=kOutput, calls=%fused_computation.36 | convolution fusion | flops 1073741824 | bytes 6815744 | tf_op jit(solution)/shard_map/dot_general | solution.py:32
  39.8 0.0 all-reduce.2.cloned.1.call-update
  39.8 0.0 reduce-scatter.2.cloned.1.call-start
  39.8 38.7 %all-reduce.2.cloned.1.call-done = f32[256,512]{1,0:T(8,128)} async-done(((f32[256,512]{1,0:T(8,128)}), f32[256,512]{1,0:T(8,128)}) %all-reduce.2.cloned.1.call-update) | async-done | bytes 524304 | tf_op jit(solution)/shard_map/psum | solution.py:41
  78.5 5.6 %fusion.17 = f32[256,4096]{1,0:T(8,128)} fusion(bf16[512,4096]{1,0:T(8,128)(2,1)} %param.7, f32[256,512]{1,0:T(8,128)} %all-reduce.2.cloned.1.call-done, bf16[256,512]{1,0:T(8,128)(2,1)S(1)} %copy-done.1), kind=kOutput, calls=%fused_computation.20 | convolution fusion | flops 1074135040 | bytes 9175040 | tf_op jit(solution)/shard_map/dot_general | solution.py:44
  84.1 0.0 reduce-scatter.2.cloned.1.call-update
  84.1 0.0 all-gather.5.cloned.1.call-start
  84.2 0.6 copy-done.3
  84.7 0.0 copy-done.4
  84.8 0.0 copy-done.5
  84.8 43.9 %reduce-scatter.2.cloned.1.call-done = f32[64,4096]{1,0:T(8,128)} async-done(((f32[256,4096]{1,0:T(8,128)}), f32[64,4096]{1,0:T(8,128)}) %reduce-scatter.2.cloned.1.call-update) | async-done | bytes 1048592 | tf_op jit(solution)/shard_map/reduce_scatter | solution.py:43
  128.7 2.6 fusion.16
  131.2 0.0 all-gather.5.cloned.1.call-update
  131.3 6.5 %copy.17 = bf16[512,4096]{0,1:T(8,128)(2,1)} copy(bf16[512,4096]{1,0:T(8,128)(2,1)} %param.7) | data formatting | bytes 8388608 | tf_op jit(solution)/shard_map/reshape | solution.py:62
  137.8 0.1 dynamic_slice.7
  137.9 16.1 %all-gather.5.cloned.1.call-done = bf16[256,4096]{1,0:T(8,128)(2,1)} async-done(((bf16[64,4096]{1,0:T(8,128)(2,1)}), bf16[256,4096]{1,0:T(8,128)(2,1)}) %all-gather.5.cloned.1.call-update) | async-done | bytes 2097168 | tf_op jit(solution)/shard_map/all_gather | solution.py:63
  154.0 4.1 %fusion.4 = f32[8,256,512]{2,1,0:T(8,128)S(1)} fusion(bf16[512,8,512]{0,2,1:T(8,128)(2,1)} %bitcast.23, bf16[32,8,8,512]{3,2,1,0:T(8,128)(2,1)} %bitcast.25), kind=kOutput, calls=%fused_computation.5 | convolution fusion | flops 1073741824 | bytes 10485760 | tf_op jit(solution)/shard_map/kta,pta->tkp/dot_general | solution.py:64
  158.1 6.3 %fusion = f32[6,256,512]{2,0,1:T(8,128)} fusion(f32[8,256,512]{2,1,0:T(8,128)S(1)} %fusion.4, s32[8]{0:T(128)S(1)} %dynamic_slice.7, s32[6]{0:T(128)S(1)} %iota_add_fusion.1), kind=kOutput, calls=%fused_computation | convolution fusion | flops 75497520 | bytes 7340088 | tf_op jit(solution)/shard_map/st,tkp->skp/dot_general | solution.py:70
  164.3 5.0 %all-to-all-start = ((f32[6,256,512]{2,0,1:T(8,128)}), f32[6,256,512]{2,0,1:T(8,128)}, u32[]{:S(2)}, u32[]{:S(2)}) async-start(f32[6,256,512]{2,0,1:T(8,128)} %fusion), calls=%async_computation.1 | async-start | bytes 8388608 | tf_op jit(solution)/shard_map/all_to_all | solution.py:71
  169.4 0.1 reshape.46
  169.4 0.1 slice_reduce_fusion
  169.6 0.1 iota_add_fusion
  169.6 0.1 add.83
  169.7 93.3 %all-to-all-done = f32[6,256,512]{2,0,1:T(8,128)} async-done(((f32[6,256,512]{2,0,1:T(8,128)}), f32[6,256,512]{2,0,1:T(8,128)}, u32[]{:S(2)}, u32[]{:S(2)}) %all-to-all-start) | async-done | bytes 3145760 | tf_op jit(solution)/shard_map/all_to_all | solution.py:71
  263.1 4.0 %copy.11 = f32[6,4,64,512]{3,2,0,1:T(8,128)S(1)} copy(f32[6,4,64,512]{3,0,2,1:T(8,128)} %bitcast.4) | data formatting | bytes 6291456 | tf_op jit(solution)/shard_map/all_to_all | solution.py:71
  267.1 3.7 %fusion.25 = (f32[64,512]{1,0:T(8,128)S(1)}, f32[22,64,512]{2,0,1:T(8,128)S(1)}) fusion(f32[24,64,512]{2,1,0:T(8,128)S(1)} %bitcast.24, s32[24]{0:T(128)S(1)} %add.83), kind=kOutput, calls=%fused_computation.35 | convolution fusion | flops 208306704 | bytes 6160480 | tf_op jit(solution)/shard_map/cj,jkp->ckp/dot_general | solution.py:75
  270.8 0.6 add_convert_fusion
  271.4 1.6 copy.13
  (12 shorter events, 0.1 us)
Async XLA Ops:
  7.2 27.7 %all-gather.3.cloned.1.call-start = ((), (), s32[]{:S(2)}) async-start(), calls=%async_computation.2 | async-start | bytes 2621440 | tf_op jit(solution)/shard_map/all_gather | solution.py:33
  7.9 70.6 %copy-start.1 = (bf16[256,512]{1,0:T(8,128)(2,1)S(1)}, bf16[256,512]{1,0:T(8,128)(2,1)}, u32[]{:S(2)}) copy-start(bf16[256,512]{1,0:T(8,128)(2,1)} %param.9) | copy-start | bytes 786436
  7.9 70.6 %all-reduce.2.cloned.1.call-start = ((), (), s32[]{:S(2)}) async-start(), calls=%async_computation.3 | async-start | bytes 1048576 | tf_op jit(solution)/shard_map/psum | solution.py:41
  39.8 88.9 %reduce-scatter.2.cloned.1.call-start = ((), (), s32[]{:S(2)}) async-start(), calls=%async_computation.4 | async-start | bytes 5242880 | tf_op jit(solution)/shard_map/reduce_scatter | solution.py:43
  84.1 0.7 copy-start.3
  84.1 0.7 copy-start.4
  84.1 0.7 copy-start.5
  84.1 44.6 %copy-start = (bf16[64,4096]{1,0:T(8,128)(2,1)S(1)}, bf16[64,4096]{1,0:T(8,128)(2,1)}, u32[]{:S(2)}) copy-start(bf16[64,4096]{1,0:T(8,128)(2,1)} %param.8) | copy-start | bytes 1572868
  84.1 69.9 %all-gather.5.cloned.1.call-start = ((), (), s32[]{:S(2)}) async-start(), calls=%async_computation.5 | async-start | bytes 2621440 | tf_op jit(solution)/shard_map/all_gather | solution.py:63
  131.3 6.5 %copy-start.2 = (s32[32]{0:T(128)S(1)}, s32[32]{0:T(128)}, u32[]{:S(2)}) copy-start(s32[32]{0:T(128)} %param.13) | copy-start | bytes 388
  164.3 98.7 %all-to-all-start = ((f32[6,256,512]{2,0,1:T(8,128)}), f32[6,256,512]{2,0,1:T(8,128)}, u32[]{:S(2)}, u32[]{:S(2)}) async-start(f32[6,256,512]{2,0,1:T(8,128)} %fusion), calls=%async_computation.1 | async-start | bytes 8388608 | tf_op jit(solution)/shard_map/all_to_all | solution.py:71
Sparse Core Ops, SparseCore 0:
  9.5 25.2 all-gather.2
  39.9 38.5 all-reduce.1
  84.3 44.3 reduce-scatter.1
  131.4 22.5 all-gather.4
where the time goes:
time: 280 us; the launch traced here: 279 us
  waiting for transfers between devices  220 us (79%)
  matrix products  24.5 us (9%)
  between operations  13.8 us (5%)
  local copies, waits for them, and re-layouts  13 us (5%)
  starting transfers between devices  5.18 us (2%)
  other arithmetic  3.29 us (1%)
    all_to_all x1, waiting for transfers between devices, per_device(): lax.all_to_all(local_sums, 'mk', split_axis=1, concat_axis=0, tiled=True)  93.3 us
    reduce_scatter x1, waiting for transfers between devices, per_device(): lax.psum_scatter(jnp.dot(residual, genotypes, preferred_element_type=jnp....  43.9 us
    psum x1, waiting for transfers between devices, per_device(): prediction = lax.psum(partial_pred, 'mk')  38.7 us
    all_gather x1, waiting for transfers between devices, per_device(): lax.all_gather(estimate, ('pp', 'sub'), axis=0, tiled=True)  26.9 us
    all_gather x1, waiting for transfers between devices, per_device(): shard_rows = lax.all_gather(updated, ('pp', 'sub'), axis=0, tiled=True)  16.1 us
    reshape x1, local copies, waits for them, and re-layouts, per_device(): geno_tiles = genotypes.reshape(people_dev, tile_dev, TILE)  6.48 us
    dot_general x1, matrix products, per_device(): jnp.einsum('st,tkp->skp', member, tile_terms, precision=lax.Precision.HIG...  6.27 us
  transfers between devices with their start and end apart: 5, of which 5 were waited for; matrix products, arithmetic and copies ran while one was open for 2% of the time, Pallas kernels for 0%

commit v1 on v0

v1 whole, which is shorter than its diff:
```python
import functools
import math

import jax
import jax.numpy as jnp
from jax import lax
from jax.experimental import pallas as pl
from jax.experimental.pallas import tpu as pltpu
from jax.sharding import PartitionSpec as P

CHROMS = 22
TILE = 512
SPAN = 6
CHUNKS = 4
F32 = jnp.float32
BF16 = jnp.bfloat16
NT = (((1,), (1,)), ((), ()))


def column(row):
    n = row.shape[1]
    at = lax.broadcasted_iota(jnp.int32, (n, n), 0)
    to = lax.broadcasted_iota(jnp.int32, (n, n), 1)
    return jnp.sum(jnp.where(at == to, jnp.broadcast_to(row, (n, n)), 0.0), axis=1, keepdims=True)


def kernel(dims, tc_ref, geno_hbm, est_hbm, phen_ref, prior_ref, slab_ref, noise_ref,
           upd_ref, loco_ref,
           geno, estbuf, pown, pbuf, precv, rbuf, sbuf, c1send, c1recv, c2send, c2recv,
           ubuf, tbuf, ebuf,
           lsem, ax_s, ax_r, ap_s, ap_r, bz_s, bz_r, rz_s, rz_r, c1_s, c1_r, c2_s, c2_r,
           dx_s, dx_r, dp_s, dp_r, ez_s, ez_r, *erecv):
    n_mk, n_pp, chunks, rows, rb, share, g, people, marks, marker_root, people_root = dims
    n_sh = n_pp * 2
    tile_dev = marks // TILE
    x, s, z = lax.axis_index("pp"), lax.axis_index("sub"), lax.axis_index("mk")
    other = 1 - s
    me = x * 2 + s
    partner = {"sub": other}

    def xid(d):
        return lax.rem(x + d, n_pp)

    def xback(d):
        return lax.rem(x + n_pp - d, n_pp)

    def zid(d):
        return lax.rem(z + d, n_mk)

    def remote(src, dst, send, recv, where):
        return pltpu.make_async_remote_copy(
            src_ref=src, dst_ref=dst, send_sem=send, recv_sem=recv,
            device_id=where, device_id_type=pl.DeviceIdType.MESH)

    started = []

    def go(copy):
        copy.start()
        started.append(copy)
        return copy

    load_geno = pltpu.make_async_copy(geno_hbm, geno, lsem.at[0])
    load_geno.start()
    own_loads = []
    for c in range(chunks):
        own = pltpu.make_async_copy(est_hbm.at[pl.ds(c * rb, rb)], estbuf.at[c, me], lsem.at[1 + c])
        own.start()
        own_loads.append(own)

    barrier = pltpu.get_barrier_semaphore()
    peers = [partner] + [{"pp": xid(d)} for d in range(1, n_pp)] + [{"mk": zid(d)} for d in range(1, n_mk)]
    for peer in peers:
        pl.semaphore_signal(barrier, inc=1, device_id=peer, device_id_type=pl.DeviceIdType.MESH)
    pl.semaphore_wait(barrier, len(peers))

    copies = {}

    def gather_start(kind, c, src, buf, xs, xr, ps, pr):
        copies[kind, c, "x"] = [
            go(remote(src, buf.at[c, me], xs.at[c, d - 1], xr.at[c, d - 1], {"pp": xid(d)}))
            for d in range(1, n_pp)]
        copies[kind, c, "p"] = [go(remote(src, buf.at[c, me], ps.at[c, 0], pr.at[c, 0], partner))]

    def gather_forward(kind, c, buf, ps, pr):
        for d in range(1, n_pp):
            copies[kind, c, "x"][d - 1].wait_recv()
            origin = xback(d) * 2 + s
            copies[kind, c, "p"].append(
                go(remote(buf.at[c, origin], buf.at[c, origin], ps.at[c, d], pr.at[c, d], partner)))

    def gather_finish(kind, c):
        for copy in copies[kind, c, "p"]:
            copy.wait_recv()

    slab, noise = column(slab_ref[...]), column(noise_ref[...])
    spread = slab + noise
    base = column(prior_ref[...]) + 0.5 * jnp.log(noise / spread)
    curve = 1.0 / noise - 1.0 / spread
    shrink = slab / spread

    first = tc_ref[z * tile_dev]
    member = [[jnp.where(tc_ref[z * tile_dev + t] == first + k, 1.0, 0.0).astype(F32)
               for t in range(tile_dev)] for k in range(SPAN)]

    def a0(c):
        gather_start("a", c, est_hbm.at[pl.ds(c * rb, rb)], estbuf, ax_s, ax_r, ap_s, ap_r)

    def a1(c):
        gather_forward("a", c, estbuf, ap_s, ap_r)

    def a2(c):
        if c == 0:
            load_geno.wait()
        own_loads[c].wait()
        gather_finish("a", c)
        pred = lax.dot_general(estbuf[c].reshape(n_sh * rb, marks), geno[...], NT,
                               preferred_element_type=F32)
        pown[c] = pred.reshape(n_mk, g, people)
        pbuf[c] = pred.astype(BF16).reshape(n_mk, g, people)
        copies["b", c] = [
            go(remote(pbuf.at[c, zid(d)], precv.at[c, d - 1], bz_s.at[c, d - 1], bz_r.at[c, d - 1], {"mk": zid(d)}))
            for d in range(1, n_mk)]

    def phen_rows(c):
        return phen_ref[pl.ds(pl.multiple_of(z * share + c * g, g), g), :].astype(F32)

    def b1(c):
        total = pown[c, z]
        for d in range(1, n_mk):
            copies["b", c][d - 1].wait_recv()
            total = total + precv[c, d - 1].astype(F32)
        rbuf[c, z] = (phen_rows(c) - total).astype(BF16)
        copies["r", c] = [
            go(remote(rbuf.at[c, z], rbuf.at[c, z], rz_s.at[c, d - 1], rz_r.at[c, d - 1], {"mk": zid(d)}))
            for d in range(1, n_mk)]

    def b2(c):
        for copy in copies["r", c]:
            copy.wait_recv()
        residual = rbuf[c].reshape(n_sh * rb, people)
        for j in range(marks // TILE):
            cols = pl.ds(j * TILE, TILE)
            sbuf[c, :, :, cols] = jnp.dot(residual, geno[:, cols], preferred_element_type=F32).reshape(n_sh, rb, TILE)
        for q in range(n_pp):
            c1send[c, q] = sbuf[c, q * 2 + other].astype(BF16)
        copies["c1", c] = go(remote(c1send.at[c], c1recv.at[c], c1_s.at[c], c1_r.at[c], partner))

    def c2(c):
        copies["c1", c].wait_recv()
        copies["c2", c] = []
        for d in range(1, n_pp):
            q = xid(d)
            c2send[c, d - 1] = (sbuf[c, q * 2 + s] + c1recv[c, q].astype(F32)).astype(BF16)
            copies["c2", c].append(
                go(remote(c2send.at[c, d - 1], c2recv.at[c, d - 1], c2_s.at[c, d - 1], c2_r.at[c, d - 1], {"pp": q})))

    def c3(c):
        for copy in copies["c2", c]:
            copy.wait_recv()
        at = slice(c * rb, (c + 1) * rb)
        scores = sbuf[c, me] + c1recv[c, x].astype(F32)
        for d in range(1, n_pp):
            scores = scores + c2recv[c, d - 1].astype(F32)
        observed = marker_root * estbuf[c, me].astype(F32) + scores * (1.0 / people_root)
        log_odds = base[at] + 0.5 * observed * observed * curve[at]
        posterior = jax.nn.sigmoid(log_odds) * shrink[at] * observed
        new = (posterior * (1.0 / marker_root)).astype(BF16)
        ubuf[c, me] = new
        upd_ref[at, :] = new
        gather_start("d", c, ubuf.at[c, me], ubuf, dx_s, dx_r, dp_s, dp_r)

    def d1(c):
        gather_forward("d", c, ubuf, dp_s, dp_r)

    def d2(c):
        gather_finish("d", c)
        for t in range(tile_dev):
            cols = pl.ds(t * TILE, TILE)
            tbuf[t] = lax.dot_general(ubuf[c, :, :, cols].reshape(n_sh * rb, TILE), geno[:, cols], NT,
                                      preferred_element_type=F32).reshape(n_mk, g, people)
        for b in range(n_mk):
            for k in range(SPAN):
                acc = tbuf[0, b] * member[k][0]
                for t in range(1, tile_dev):
                    acc = acc + tbuf[t, b] * member[k][t]
                ebuf[c, b, k] = acc.astype(BF16)
        copies["e", c] = [
            go(remote(ebuf.at[c, zid(d)], erecv[c].at[d - 1], ez_s.at[c, d - 1], ez_r.at[c, d - 1], {"mk": zid(d)}))
            for d in range(1, n_mk)]

    def e1(c):
        for copy in copies["e", c]:
            copy.wait_recv()
        total = jnp.zeros((g, people), F32)
        for k in range(SPAN):
            total = total + ebuf[c, z, k].astype(F32)
            for d in range(1, n_mk):
                total = total + erecv[c][d - 1, k].astype(F32)
        rest = phen_rows(c) - total
        for q in range(CHROMS):
            value = rest
            for d in range(n_mk):
                source = lax.rem(z + n_mk - d, n_mk)
                slot = q - tc_ref[source * tile_dev]
                held = jnp.where((slot >= 0) & (slot < SPAN), 1.0, 0.0).astype(F32)
                slot = jnp.clip(slot, 0, SPAN - 1)
                block = ebuf[c, z, slot] if d == 0 else erecv[c][d - 1, slot]
                value = value + block.astype(F32) * held
            loco_ref[q, c * g:(c + 1) * g, :] = value.astype(BF16)

    stages = [a1, a2, b1, b2, c2, c3, d1, d2, e1]
    for c in range(chunks):
        a0(c)
    for step in range(len(stages) + chunks - 1):
        for c in range(chunks):
            if 0 <= step - c < len(stages):
                stages[step - c](c)
    for copy in started:
        copy.wait_send()


def per_device(genotypes, estimate, phenotypes, prior_logit, slab_var, noise_var, tile_chrom):
    people, marks = genotypes.shape
    n_mk, n_pp, n_sub = lax.axis_size("mk"), lax.axis_size("pp"), lax.axis_size("sub")
    traits, rows = phenotypes.shape[0], estimate.shape[0]
    share = traits // n_mk
    assert n_sub == 2
    chunks = CHUNKS if share == rows and rows % (16 * CHUNKS) == 0 else 1
    rb, g = rows // chunks, share // chunks
    n_sh, tile_dev = n_pp * 2, marks // TILE
    dims = (n_mk, n_pp, chunks, rows, rb, share, g, people, marks,
            math.sqrt(marks * n_mk), math.sqrt(people * n_pp * n_sub))
    vmem, dma = pltpu.VMEM, pltpu.SemaphoreType.DMA
    xs, zs = n_pp - 1, n_mk - 1
    in_vmem = pl.BlockSpec(memory_space=pltpu.VMEM)
    in_any = pl.BlockSpec(memory_space=pl.ANY)
    return pl.pallas_call(
        functools.partial(kernel, dims),
        out_shape=(jax.ShapeDtypeStruct((rows, marks), BF16),
                   jax.ShapeDtypeStruct((CHROMS, share, people), BF16)),
        in_specs=[pl.BlockSpec(memory_space=pltpu.SMEM), in_any, in_any, in_vmem, in_vmem, in_vmem, in_vmem],
        out_specs=(in_vmem, in_vmem),
        scratch_shapes=[
            vmem((people, marks), BF16),
            vmem((chunks, n_sh, rb, marks), BF16),
            vmem((chunks, n_mk, g, people), F32),
            vmem((chunks, n_mk, g, people), BF16),
            vmem((chunks, zs, g, people), BF16),
            vmem((chunks, n_mk, g, people), BF16),
            vmem((chunks, n_sh, rb, marks), F32),
            vmem((chunks, n_pp, rb, marks), BF16),
            vmem((chunks, n_pp, rb, marks), BF16),
            vmem((chunks, xs, rb, marks), BF16),
            vmem((chunks, xs, rb, marks), BF16),
            vmem((chunks, n_sh, rb, marks), BF16),
            vmem((tile_dev, n_mk, g, people), F32),
            vmem((chunks, n_mk, SPAN, g, people), BF16),
            dma((1 + chunks,)),
            dma((chunks, xs)), dma((chunks, xs)), dma((chunks, n_pp)), dma((chunks, n_pp)),
            dma((chunks, zs)), dma((chunks, zs)), dma((chunks, zs)), dma((chunks, zs)),
            dma((chunks,)), dma((chunks,)), dma((chunks, xs)), dma((chunks, xs)),
            dma((chunks, xs)), dma((chunks, xs)), dma((chunks, n_pp)), dma((chunks, n_pp)),
            dma((chunks, zs)), dma((chunks, zs)),
        ] + [vmem((zs, SPAN, g, people), BF16) for _ in range(chunks)],
        compiler_params=pltpu.CompilerParams(
            collective_id=0, has_side_effects=True, vmem_limit_bytes=56 * 1024 * 1024),
    )(tile_chrom, genotypes, estimate, phenotypes,
      prior_logit.reshape(1, rows), slab_var.reshape(1, rows), noise_var.reshape(1, rows))


def solution(mesh):
    placed = (
        P(("grp", "pp", "sub"), "mk"),
        P(("grp", "pp", "sub"), "mk"),
        P("grp", ("pp", "sub")),
        P(("grp", "pp", "sub")),
        P(("grp", "pp", "sub")),
        P(("grp", "pp", "sub")),
        P("grp"),
    )
    return jax.shard_map(
        per_device,
        mesh=mesh,
        in_specs=placed,
        out_specs=(P(("grp", "pp", "sub"), "mk"), P("grp", "mk", ("pp", "sub"))),
        check_vma=False,
    )
```

time: 280 us -> 83 us (0.30)
  waiting for transfers between devices: 220 us -> 0 us
  Pallas kernels: 0 us -> 77.7 us
  matrix products: 24.5 us -> 0 us
  between operations: 13.8 us -> 0.64 us
  local copies, waits for them, and re-layouts: 13 us -> 4.47 us
  starting transfers between devices: 5.18 us -> 0 us
  other arithmetic: 3.29 us -> 0 us
    all_to_all x1 -> x0, waiting for transfers between devices: 93.3 us -> none  [per_device(): lax.all_to_all(local_sums, 'mk', split_axis=1, concat_axis=0, tiled=True)]
    pallas_call x0 -> x1, Pallas kernels: none -> 77.7 us  [per_device(): pl.pallas_call(functools.partial(kernel, dims), out_shape=(jax.ShapeDtype...]
    reduce_scatter x1 -> x0, waiting for transfers between devices: 43.9 us -> none  [per_device(): lax.psum_scatter(jnp.dot(residual, genotypes, preferred_element_type=jnp....]
    all_gather x2 -> x0, waiting for transfers between devices: 43 us -> none  [the longest x1 26.9 us: per_device(): lax.all_gather(estimate, ('pp', 'sub'), axis=0, tiled=True)]
    psum x1 -> x0, waiting for transfers between devices: 38.7 us -> none  [per_device(): prediction = lax.psum(partial_pred, 'mk')]
    dot_general x5 -> x0, matrix products: 24.5 us -> none  [the longest x1 6.27 us: per_device(): jnp.einsum('st,tkp->skp', member, tile_terms, precision=lax.Precision.HIG...]
    reshape x2 -> x0, local copies, waits for them, and re-layouts: 6.56 us -> none  [the longest x1 6.48 us: per_device(): geno_tiles = genotypes.reshape(people_dev, tile_dev, TILE)]
    all_to_all x1 -> x0, starting transfers between devices: 5.02 us -> none  [per_device(): lax.all_to_all(local_sums, 'mk', split_axis=1, concat_axis=0, tiled=True)]
  transfers between devices with their start and end apart: 5 -> 0, of which waited for: 5 -> 0; matrix products, arithmetic and copies ran while one was open for 2% -> 0% of each run, Pallas kernels for 0% -> 0%
where the time goes in v1:
time: 83 us; the launch traced here: 82.8 us
  Pallas kernels  77.7 us (94%)
  local copies, waits for them, and re-layouts  4.47 us (5%)
    pallas_call x1, Pallas kernels, per_device(): pl.pallas_call(functools.partial(kernel, dims), out_shape=(jax.ShapeDtype...  77.7 us
    unnamed x2, local copies, waits for them, and re-layouts  4.47 us

profile of v1, /device:TPU:0, one launch (start us, length us, event | category | flops | bytes accessed | tf_op | source)
XLA Modules:
  0.0 82.8 jit_solution(15699712609949606957)
XLA Ops:
  0.6 77.7 %shard_map.86 = (bf16[64,4096]{1,0:T(8,128)(2,1)}, bf16[22,64,512]{2,1,0:T(8,128)(2,1)}) custom-call(s32[32]{0:T(128)} %tc_ref.1, bf16[512,4096]{1,0:T(8,128)(2,1)} %geno_hbm.1, bf16[64,4096]{1,0:T(8,128)(2,1)} %est_hbm.1, bf16[256,512]{1,0:T(8,128)(2,1)} %phen_ref.1, f32[1,64]{1,0:T(1,128)} %bitcast.3, f32[1,64]{1,0:T(1,128)} %bitcast.4, f32[1,64]{1,0:T(1,128)} %bitcast.5), custom_call_target="tpu_custom_call" | custom-call | tf_op jit(solution)/shard_map/pallas_call | solution.py:237
  78.4 1.9 %copy.11 = bf16[64,4096]{1,0:T(8,128)(2,1)} copy(bf16[64,4096]{1,0:T(8,128)(2,1)} %get-tuple-element.4) | data formatting | bytes 1048576
  80.2 2.6 %copy.12 = bf16[22,64,512]{2,1,0:T(8,128)(2,1)} copy(bf16[22,64,512]{2,1,0:T(8,128)(2,1)} %get-tuple-element.5) | data formatting | bytes 2883584

commit v2 on v1

--- a/solution.py
+++ b/solution.py
@@ -12,6 +12,10 @@
 TILE = 512
 SPAN = 6
 CHUNKS = 4
+ORDER = [
+    [0, 10, 1, 11, 20, 2, 12, 30, 21, 3, 13, 40, 22, 31, 50, 41, 23, 32],
+    [60, 33, 70, 51, 42, 61, 71, 52, 43, 62, 80, 72, 53, 63, 73, 81, 82, 83],
+]
 F32 = jnp.float32
 BF16 = jnp.bfloat16
 NT = (((1,), (1,)), ((), ()))
@@ -25,11 +29,11 @@
 
 
 def kernel(dims, tc_ref, geno_hbm, est_hbm, phen_ref, prior_ref, slab_ref, noise_ref,
-           upd_ref, loco_ref,
+           upd_hbm, slots_hbm,
            geno, estbuf, pown, pbuf, precv, rbuf, sbuf, c1send, c1recv, c2send, c2recv,
            ubuf, tbuf, ebuf,
-           lsem, ax_s, ax_r, ap_s, ap_r, bz_s, bz_r, rz_s, rz_r, c1_s, c1_r, c2_s, c2_r,
-           dx_s, dx_r, dp_s, dp_r, ez_s, ez_r, *erecv):
+           lsem, osem, ksem, ax_s, ax_r, ap_s, ap_r, bz_s, bz_r, rz_s, rz_r, c1_s, c1_r, c2_s, c2_r,
+           dx_s, dx_r, dp_s, dp_r, ez_s, ez_r):
     n_mk, n_pp, chunks, rows, rb, share, g, people, marks, marker_root, people_root = dims
     n_sh = n_pp * 2
     tile_dev = marks // TILE
@@ -59,8 +63,14 @@
         started.append(copy)
         return copy
 
+    kept = []
+
+    def local(src, dst, sem):
+        copy = pltpu.make_async_copy(src, dst, sem)
+        copy.start()
+        kept.append(copy)
+
     load_geno = pltpu.make_async_copy(geno_hbm, geno, lsem.at[0])
-    load_geno.start()
     own_loads = []
     for c in range(chunks):
         own = pltpu.make_async_copy(est_hbm.at[pl.ds(c * rb, rb)], estbuf.at[c, me], lsem.at[1 + c])
@@ -166,8 +176,8 @@
         posterior = jax.nn.sigmoid(log_odds) * shrink[at] * observed
         new = (posterior * (1.0 / marker_root)).astype(BF16)
         ubuf[c, me] = new
-        upd_ref[at, :] = new
         gather_start("d", c, ubuf.at[c, me], ubuf, dx_s, dx_r, dp_s, dp_r)
+        local(ubuf.at[c, me], upd_hbm.at[pl.ds(c * rb, rb)], osem.at[c])
 
     def d1(c):
         gather_forward("d", c, ubuf, dp_s, dp_r)
@@ -185,38 +195,44 @@
                     acc = acc + tbuf[t, b] * member[k][t]
                 ebuf[c, b, k] = acc.astype(BF16)
         copies["e", c] = [
-            go(remote(ebuf.at[c, zid(d)], erecv[c].at[d - 1], ez_s.at[c, d - 1], ez_r.at[c, d - 1], {"mk": zid(d)}))
+            go(remote(ebuf.at[c, zid(d)], slots_hbm.at[z, :, pl.ds(c * g, g)], ez_s.at[c, d - 1], ez_r.at[c, d - 1], {"mk": zid(d)}))
             for d in range(1, n_mk)]
+        local(ebuf.at[c, z], slots_hbm.at[z, :, pl.ds(c * g, g)], ksem.at[c])
 
     def e1(c):
         for copy in copies["e", c]:
             copy.wait_recv()
-        total = jnp.zeros((g, people), F32)
-        for k in range(SPAN):
-            total = total + ebuf[c, z, k].astype(F32)
-            for d in range(1, n_mk):
-                total = total + erecv[c][d - 1, k].astype(F32)
-        rest = phen_rows(c) - total
-        for q in range(CHROMS):
-            value = rest
-            for d in range(n_mk):
-                source = lax.rem(z + n_mk - d, n_mk)
-                slot = q - tc_ref[source * tile_dev]
-                held = jnp.where((slot >= 0) & (slot < SPAN), 1.0, 0.0).astype(F32)
-                slot = jnp.clip(slot, 0, SPAN - 1)
-                block = ebuf[c, z, slot] if d == 0 else erecv[c][d - 1, slot]
-                value = value + block.astype(F32) * held
-            loco_ref[q, c * g:(c + 1) * g, :] = value.astype(BF16)
 
     stages = [a1, a2, b1, b2, c2, c3, d1, d2, e1]
     for c in range(chunks):
         a0(c)
-    for step in range(len(stages) + chunks - 1):
-        for c in range(chunks):
-            if 0 <= step - c < len(stages):
-                stages[step - c](c)
+    load_geno.start()
+    for names in (ORDER if chunks == 4 else [[k * 10 for k in range(len(stages))]]):
+        for name in names:
+            stages[name // 10](name % 10)
     for copy in started:
         copy.wait_send()
+    for copy in kept:
+        copy.wait()
+
+
+def finish(dims, tc_ref, slots_ref, upd_ref, phen_ref, new_ref, loco_ref):
+    n_mk, share, g, tile_dev = dims
+    step = pl.program_id(0)
+    new_ref[...] = upd_ref[...]
+    at = pl.multiple_of(lax.axis_index("mk") * share + step * g, g)
+    total = jnp.zeros(loco_ref.shape[1:], F32)
+    for j in range(n_mk):
+        for k in range(SPAN):
+            total = total + slots_ref[j, k].astype(F32)
+    rest = phen_ref[pl.ds(at, g), :].astype(F32) - total
+    for q in range(CHROMS):
+        value = rest
+        for j in range(n_mk):
+            slot = q - tc_ref[j * tile_dev]
+            held = jnp.where((slot >= 0) & (slot < SPAN), 1.0, 0.0).astype(F32)
+            value = value + slots_ref[j, jnp.clip(slot, 0, SPAN - 1)].astype(F32) * held
+        loco_ref[q] = value.astype(BF16)
 
 
 def per_device(genotypes, estimate, phenotypes, prior_logit, slab_var, noise_var, tile_chrom):
@@ -234,12 +250,12 @@
     xs, zs = n_pp - 1, n_mk - 1
     in_vmem = pl.BlockSpec(memory_space=pltpu.VMEM)
     in_any = pl.BlockSpec(memory_space=pl.ANY)
-    return pl.pallas_call(
+    new, slots = pl.pallas_call(
         functools.partial(kernel, dims),
         out_shape=(jax.ShapeDtypeStruct((rows, marks), BF16),
-                   jax.ShapeDtypeStruct((CHROMS, share, people), BF16)),
+                   jax.ShapeDtypeStruct((n_mk, SPAN, share, people), BF16)),
         in_specs=[pl.BlockSpec(memory_space=pltpu.SMEM), in_any, in_any, in_vmem, in_vmem, in_vmem, in_vmem],
-        out_specs=(in_vmem, in_vmem),
+        out_specs=(in_any, in_any),
         scratch_shapes=[
             vmem((people, marks), BF16),
             vmem((chunks, n_sh, rb, marks), BF16),
@@ -255,17 +271,29 @@
             vmem((chunks, n_sh, rb, marks), BF16),
             vmem((tile_dev, n_mk, g, people), F32),
             vmem((chunks, n_mk, SPAN, g, people), BF16),
-            dma((1 + chunks,)),
+            dma((1 + chunks,)), dma((chunks,)), dma((chunks,)),
             dma((chunks, xs)), dma((chunks, xs)), dma((chunks, n_pp)), dma((chunks, n_pp)),
             dma((chunks, zs)), dma((chunks, zs)), dma((chunks, zs)), dma((chunks, zs)),
             dma((chunks,)), dma((chunks,)), dma((chunks, xs)), dma((chunks, xs)),
             dma((chunks, xs)), dma((chunks, xs)), dma((chunks, n_pp)), dma((chunks, n_pp)),
             dma((chunks, zs)), dma((chunks, zs)),
-        ] + [vmem((zs, SPAN, g, people), BF16) for _ in range(chunks)],
+        ],
         compiler_params=pltpu.CompilerParams(
             collective_id=0, has_side_effects=True, vmem_limit_bytes=56 * 1024 * 1024),
     )(tile_chrom, genotypes, estimate, phenotypes,
       prior_logit.reshape(1, rows), slab_var.reshape(1, rows), noise_var.reshape(1, rows))
+    return pl.pallas_call(
+        functools.partial(finish, (n_mk, share, g, tile_dev)),
+        grid=(chunks,),
+        out_shape=(jax.ShapeDtypeStruct((rows, marks), BF16),
+                   jax.ShapeDtypeStruct((CHROMS, share, people), BF16)),
+        in_specs=[pl.BlockSpec(memory_space=pltpu.SMEM),
+                  pl.BlockSpec((n_mk, SPAN, g, people), lambda i: (0, 0, i, 0)),
+                  pl.BlockSpec((rb, marks), lambda i: (i, 0)),
+                  pl.BlockSpec((traits, people), lambda i: (0, 0))],
+        out_specs=(pl.BlockSpec((rb, marks), lambda i: (i, 0)),
+                   pl.BlockSpec((CHROMS, g, people), lambda i: (0, i, 0))),
+    )(tile_chrom, slots, new, phenotypes)
 
 
 def solution(mesh):

time: 83 us -> 80.1 us (0.965)
  local copies, waits for them, and re-layouts: 4.47 us -> 0 us
  Pallas kernels: 77.7 us -> 79.2 us
    pallas_call x0 -> x1, Pallas kernels: none -> 4.5 us  [per_device(): pl.pallas_call(functools.partial(finish, (n_mk, share, g, tile_dev)), gri...]
    unnamed x2 -> x0, local copies, waits for them, and re-layouts: 4.47 us -> none
    pallas_call x1, Pallas kernels: 77.7 us -> 74.7 us  [per_device(): pl.pallas_call(functools.partial(kernel, dims), out_shape=(jax.ShapeDtype...]
where the time goes in v2:
time: 80.1 us; the launch traced here: 79.9 us
  Pallas kernels  79.2 us (99%)
    pallas_call x1, Pallas kernels, per_device(): pl.pallas_call(functools.partial(kernel, dims), out_shape=(jax.ShapeDtype...  74.7 us
    pallas_call x1, Pallas kernels, per_device(): pl.pallas_call(functools.partial(finish, (n_mk, share, g, tile_dev)), gri...  4.5 us

profile of v2, /device:TPU:0, one launch (start us, length us, event | category | flops | bytes accessed | tf_op | source)
XLA Modules:
  0.0 79.9 jit_solution(292464062523850136)
XLA Ops:
  0.6 74.7 %shard_map.86 = (bf16[64,4096]{1,0:T(8,128)(2,1)}, bf16[4,6,64,512]{3,2,1,0:T(8,128)(2,1)}) custom-call(s32[32]{0:T(128)} %tc_ref.3, bf16[512,4096]{1,0:T(8,128)(2,1)} %geno_hbm.1, bf16[64,4096]{1,0:T(8,128)(2,1)} %est_hbm.1, bf16[256,512]{1,0:T(8,128)(2,1)} %phen_ref.3, f32[1,64]{1,0:T(1,128)} %bitcast.3, f32[1,64]{1,0:T(1,128)} %bitcast.4, f32[1,64]{1,0:T(1,128)} %bitcast.5), custom_call_target="tpu_custom_call" | custom-call | tf_op jit(solution)/shard_map/pallas_call | solution.py:253
  75.4 4.5 %shard_map.87 = (bf16[64,4096]{1,0:T(8,128)(2,1)}, bf16[22,64,512]{2,1,0:T(8,128)(2,1)}) custom-call(s32[32]{0:T(128)} %tc_ref.3, bf16[4,6,64,512]{3,2,1,0:T(8,128)(2,1)} %get-tuple-element.4.slots_ref, bf16[64,4096]{1,0:T(8,128)(2,1)} %get-tuple-element.5.upd_ref, bf16[256,512]{1,0:T(8,128)(2,1)} %phen_ref.3), custom_call_target="tpu_custom_call" | custom-call | tf_op jit(solution)/shard_map/pallas_call | solution.py:285

commit v3 on v2

--- a/solution.py
+++ b/solution.py
@@ -13,8 +13,8 @@
 SPAN = 6
 CHUNKS = 4
 ORDER = [
-    [0, 10, 1, 11, 20, 2, 12, 30, 21, 3, 13, 40, 22, 31, 50, 41, 23, 32],
-    [60, 33, 70, 51, 42, 61, 71, 52, 43, 62, 80, 72, 53, 63, 73, 81, 82, 83],
+    [0, 10, 1, 11, 2, 20, 12, 3, 21, 13, 30, 22, 31, 40, 23, 41, 32, 50],
+    [42, 33, 51, 43, 60, 70, 52, 61, 71, 53, 62, 72, 63, 73, 80, 81, 82, 83],
 ]
 F32 = jnp.float32
 BF16 = jnp.bfloat16

time: 80.1 us -> 79.6 us (level)
  Pallas kernels: 79.2 us -> 78.1 us
    pallas_call x1, Pallas kernels: 74.7 us -> 73.6 us  [per_device(): pl.pallas_call(functools.partial(kernel, dims), out_shape=(jax.ShapeDtype...]
where the time goes in v3:
time: 79.6 us; the launch traced here: 78.8 us
  Pallas kernels  78.1 us (98%)
    pallas_call x1, Pallas kernels, per_device(): pl.pallas_call(functools.partial(kernel, dims), out_shape=(jax.ShapeDtype...  73.6 us
    pallas_call x1, Pallas kernels, per_device(): pl.pallas_call(functools.partial(finish, (n_mk, share, g, tile_dev)), gri...  4.5 us

profile of v3, /device:TPU:0, one launch (start us, length us, event | category | flops | bytes accessed | tf_op | source)
XLA Modules:
  0.0 78.8 jit_solution(9765751734046807495)
XLA Ops:
  0.6 73.6 %shard_map.86 = (bf16[64,4096]{1,0:T(8,128)(2,1)}, bf16[4,6,64,512]{3,2,1,0:T(8,128)(2,1)}) custom-call(s32[32]{0:T(128)} %tc_ref.3, bf16[512,4096]{1,0:T(8,128)(2,1)} %geno_hbm.1, bf16[64,4096]{1,0:T(8,128)(2,1)} %est_hbm.1, bf16[256,512]{1,0:T(8,128)(2,1)} %phen_ref.3, f32[1,64]{1,0:T(1,128)} %bitcast.3, f32[1,64]{1,0:T(1,128)} %bitcast.4, f32[1,64]{1,0:T(1,128)} %bitcast.5), custom_call_target="tpu_custom_call" | custom-call | tf_op jit(solution)/shard_map/pallas_call | solution.py:253
  74.3 4.5 %shard_map.87 = (bf16[64,4096]{1,0:T(8,128)(2,1)}, bf16[22,64,512]{2,1,0:T(8,128)(2,1)}) custom-call(s32[32]{0:T(128)} %tc_ref.3, bf16[4,6,64,512]{3,2,1,0:T(8,128)(2,1)} %get-tuple-element.4.slots_ref, bf16[64,4096]{1,0:T(8,128)(2,1)} %get-tuple-element.5.upd_ref, bf16[256,512]{1,0:T(8,128)(2,1)} %phen_ref.3), custom_call_target="tpu_custom_call" | custom-call | tf_op jit(solution)/shard_map/pallas_call | solution.py:285
